TPU v7x, 32 devices: a whole 2x2x4 slice. The times are simulated.
32 devices in a mesh: grp: 2 (over x), tok: 8 (over z, y), lay: 2 (over core).
Axes of the slice: x: 2, y: 2, z: 4, core: 2. Of those that a mesh axis runs over, the one named last changes fastest.
Arguments:
- acts: bfloat16 [3072, 16, 128], P(('grp', 'tok'), 'lay'), parts along dimension 0, may hold values from -0.5 to 0.5
- grads: bfloat16 [3072, 16, 128], P(('grp', 'tok'), 'lay'), parts along dimension 0, may hold values from -0.5 to 0.5
- losses: bfloat16 [3072, 128], P(('grp', 'tok')), parts along dimension 0, may hold values from -6 to 6
- sources: int32 [3072], P(('grp', 'tok')), parts along dimension 0, may hold values from 0 to 7
Outputs:
- scores: float32 [3072, 128], P(('grp', 'tok', 'lay')), parts along dimension 0
There are 2 independent parts, one for each index of `grp`. A program takes and returns all parts, laid end to end along the dimension named above; each array names one. Nothing has to cross between parts.
All inputs are finite; a program needn't handle non-finite values.
Results may differ from a plain program's by a relative error of at most 0.011.
Values may be sent and summed in bfloat16 or wider, within the bound.
A program may use at most 128 MiB of HBM per device.

v0:
```python
import math

import jax
import jax.numpy as jnp
from jax import lax
from jax.sharding import PartitionSpec as P

LAYERS = 16


def pair_block(own_acts, own_grads, own_ids, other_acts, other_grads, other_ids):
    total = jnp.zeros((own_acts.shape[0], other_acts.shape[0]), jnp.float32)
    for layer in range(own_acts.shape[1]):
        gram_act = jnp.einsum(
            "ik,jk->ij",
            own_acts[:, layer, :],
            other_acts[:, layer, :],
            preferred_element_type=jnp.float32,
        )
        gram_grad = jnp.einsum(
            "ik,jk->ij",
            own_grads[:, layer, :],
            other_grads[:, layer, :],
            preferred_element_type=jnp.float32,
        )
        total = total + gram_act * gram_grad
    keep = own_ids[:, None] != other_ids[None, :]
    return jnp.where(keep, total, jnp.zeros_like(total)).astype(jnp.bfloat16)


def on_device(acts, grads, losses, sources):
    block = acts.shape[0]
    count = lax.axis_size("tok")
    me = lax.axis_index("tok")
    all_ids = lax.all_gather(sources, "tok", axis=0, tiled=True)
    own_ids = lax.dynamic_slice_in_dim(all_ids, me * block, block)
    piece_acts = lax.all_gather(acts, "tok", axis=0, tiled=True)
    piece_grads = lax.all_gather(grads, "tok", axis=0, tiled=True)
    piece_losses = lax.all_gather(losses, "tok", axis=0, tiled=True)
    weights = pair_block(acts, grads, own_ids, piece_acts, piece_grads, all_ids)
    partial_scores = jnp.dot(weights, piece_losses, preferred_element_type=jnp.float32)
    summed = lax.psum_scatter(
        partial_scores.astype(jnp.bfloat16), "lay", scatter_dimension=0, tiled=True
    ).astype(jnp.float32)
    scale = 1.0 / math.sqrt(count * block * LAYERS)
    return summed * scale


def solution(mesh):
    placed = (
        P(("grp", "tok"), "lay", None),
        P(("grp", "tok"), "lay", None),
        P(("grp", "tok"), None),
        P(("grp", "tok")),
    )
    return jax.shard_map(
        on_device,
        mesh=mesh,
        in_specs=placed,
        out_specs=P(("grp", "tok", "lay"), None),
        check_vma=False,
    )
```

profile of v0, /device:TPU:0, one launch (start us, length us, event | category | flops | bytes accessed | tf_op | source)
XLA Modules:
  0.0 161.1 jit_solution(6627939347339312757)
XLA Ops:
  6.6 1.8 %copy.5 = bf16[192,8,128]{2,0,1:T(8,128)(2,1)} copy(bf16[192,8,128]{2,1,0:T(8,128)(2,1)} %param.4) | data formatting | bytes 786432 | tf_op args[0]
  8.5 0.0 all-gather.5.cloned.1.call-start
  8.5 0.8 copy.7
  9.4 0.0 reduce-scatter.2.cloned.1.call-start
  9.4 0.6 dynamic-slice
  10.7 0.3 dynamic-update-slice
  11.0 13.3 %all-reduce = s32[1536]{0:T(1024)S(1)} all-reduce(s32[1536]{0:T(1024)S(1)} %dynamic-update-slice), channel_id=1, replica_groups=mesh['grp'=2,'tok'=8,'lay'=2] {'tok'}, use_global_device_ids=true, to_apply=%add | all-reduce | flops 1536 | bytes 12288
  24.3 0.1 dynamic_slice.3
  24.4 34.1 %all_gather.15 = bf16[1536,128]{1,0:T(8,128)(2,1)} all-gather(bf16[192,128]{1,0:T(8,128)(2,1)S(1)} %copy-done.9), channel_id=1, replica_groups=mesh['grp'=2,'tok'=8,'lay'=2] {'tok'}, dimensions={0}, use_global_device_ids=true | all-gather | bytes 442368 | tf_op jit(solution)/shard_map/all_gather | solution.py:39
  58.5 17.5 %all-gather.3.cloned.1.call-done = bf16[1536,8,128]{2,0,1:T(8,128)(2,1)} async-done(((bf16[192,8,128]{2,0,1:T(8,128)(2,1)}), bf16[1536,8,128]{2,0,1:T(8,128)(2,1)}) %all-gather.3.cloned.1.call-update) | async-done | bytes 3145744 | tf_op jit(solution)/shard_map/all_gather | solution.py:37
  76.0 2.5 %fusion.21 = f32[192,1536]{1,0:T(8,128)} fusion(bf16[1536,8,128]{2,0,1:T(8,128)(2,1)} %all-gather.3.cloned.1.call-done, bf16[192,8,128]{2,0,1:T(8,128)(2,1)S(1)} %copy-done.5), kind=kOutput, calls=%fused_computation.43 | convolution fusion | flops 75497472 | bytes 1622016 | tf_op jit(solution)/shard_map/ik,jk->ij/dot_general | solution.py:14
  78.5 2.4 %fusion.22 = f32[192,1536]{1,0:T(8,128)} fusion(bf16[1536,8,128]{2,0,1:T(8,128)(2,1)} %all-gather.3.cloned.1.call-done, bf16[192,8,128]{2,0,1:T(8,128)(2,1)S(1)} %copy-done.5), kind=kOutput, calls=%fused_computation.46 | convolution fusion | flops 75497472 | bytes 1622016 | tf_op jit(solution)/shard_map/ik,jk->ij/dot_general | solution.py:14
  80.8 1.3 fusion.20
  82.2 1.4 fusion.19
  83.6 1.3 fusion.18
  84.9 0.3 fusion.17
  85.2 0.3 fusion.16
  85.5 1.1 fusion.15
  86.7 51.0 %all-gather.5.cloned.1.call-done = bf16[1536,8,128]{2,0,1:T(8,128)(2,1)} async-done(((bf16[192,8,128]{2,0,1:T(8,128)(2,1)}), bf16[1536,8,128]{2,0,1:T(8,128)(2,1)}) %all-gather.5.cloned.1.call-update) | async-done | bytes 3145744 | tf_op jit(solution)/shard_map/all_gather | solution.py:38
  137.7 1.9 %convolution_multiply_fusion.6 = f32[192,1536]{1,0:T(8,128)S(1)} fusion(f32[192,1536]{1,0:T(8,128)} %fusion.21, bf16[1536,8,128]{2,0,1:T(8,128)(2,1)} %all-gather.5.cloned.1.call-done, bf16[192,8,128]{2,0,1:T(8,128)(2,1)} %copy.7), kind=kOutput, calls=%fused_computation.6 | convolution fusion | flops 75792384 | bytes 2801664 | tf_op jit(solution)/shard_map/ik,jk->ij/dot_general | solution.py:20
  139.6 1.4 fusion
  141.0 0.2 copy-done.2
  141.2 0.3 fusion.1
  141.5 0.9 copy-done.1
  142.5 0.3 fusion.2
  142.8 0.9 copy-done
  143.8 0.3 fusion.3
  144.1 0.3 fusion.4
  144.4 0.3 fusion.5
  144.7 2.3 %fusion.11 = bf16[192,128]{1,0:T(8,128)(2,1)} fusion(bf16[1536,128]{1,0:T(8,128)(2,1)} %all_gather.15, f32[192,1536]{1,0:T(8,128)S(1)} %fusion.5, f32[192,1536]{1,0:T(8,128)S(1)} %fusion.15, s32[1536]{0:T(1024)S(1)} %all-reduce, s32[192]{0:T(256)S(1)} %dynamic_slice.3, bf16[1536,8,128]{2,0,1:T(8,128)(2,1)} %all-gather.5.cloned.1.call-done, ...), kind=kOutput, calls=%fused_computation.19 | convolution fusion | flops 152494080 | bytes 3250944 | tf_op jit(solution)/shard_map/dot_general | solution.py:41
  147.0 6.2 %reduce-scatter.2.cloned.1.call-done = bf16[96,128]{1,0:T(8,128)(2,1)} async-done(((bf16[192,128]{1,0:T(8,128)(2,1)}), bf16[96,128]{1,0:T(8,128)(2,1)}) %reduce-scatter.2.cloned.1.call-update) | async-done | bytes 24592 | tf_op jit(solution)/shard_map/reduce_scatter | solution.py:42
  153.2 1.4 convert_multiply_fusion
  (26 shorter events, 0.1 us)
Async XLA Ops:
  6.5 2.9 %copy-start.11 = (u32[32]{0:T(128)S(1)}, u32[32]{0:T(128)}, u32[]{:S(2)}) copy-start(u32[32]{0:T(128)} %constant.18) | copy-start | bytes 388
  6.5 2.0 %copy-start.8 = (bf16[192,8,128]{2,1,0:T(8,128)(2,1)S(1)}, bf16[192,8,128]{2,1,0:T(8,128)(2,1)}, u32[]{:S(2)}) copy-start(bf16[192,8,128]{2,1,0:T(8,128)(2,1)} %param.5) | copy-start | bytes 1179652
  6.5 4.1 %copy-start.10 = (s32[192]{0:T(256)S(1)}, s32[192]{0:T(256)}, u32[]{:S(2)}) copy-start(s32[192]{0:T(256)} %param.7) | copy-start | bytes 2308
  6.5 17.8 %copy-start.9 = (bf16[192,128]{1,0:T(8,128)(2,1)S(1)}, bf16[192,128]{1,0:T(8,128)(2,1)}, u32[]{:S(2)}) copy-start(bf16[192,128]{1,0:T(8,128)(2,1)} %param.6) | copy-start | bytes 147460
  6.5 69.4 %all-gather.3.cloned.1.call-start = ((), (), s32[]{:S(2)}) async-start(), calls=%async_computation.1 | async-start | bytes 3538944 | tf_op jit(solution)/shard_map/all_gather | solution.py:37
  8.4 67.5 %copy-start.5 = (bf16[192,8,128]{2,0,1:T(8,128)(2,1)S(1)}, bf16[192,8,128]{2,0,1:T(8,128)(2,1)}, u32[]{:S(2)}) copy-start(bf16[192,8,128]{2,0,1:T(8,128)(2,1)} %copy.5) | copy-start | bytes 1179652
  8.5 129.2 %all-gather.5.cloned.1.call-start = ((), (), s32[]{:S(2)}) async-start(), calls=%async_computation.2 | async-start | bytes 3538944 | tf_op jit(solution)/shard_map/all_gather | solution.py:38
  9.4 143.8 %reduce-scatter.2.cloned.1.call-start = ((), (), s32[]{:S(2)}) async-start(), calls=%async_computation.3 | async-start | bytes 73728 | tf_op jit(solution)/shard_map/reduce_scatter | solution.py:42
  76.0 4.9 %copy-start.6 = (bf16[1536,8,128]{2,0,1:T(8,128)(2,1)S(1)}, bf16[1536,8,128]{2,0,1:T(8,128)(2,1)}, u32[]{:S(2)}) copy-start(bf16[1536,8,128]{2,0,1:T(8,128)(2,1)} %all-gather.3.cloned.1.call-done) | copy-start | bytes 9437188
  137.7 1.9 %copy-start.3 = (f32[192,1536]{1,0:T(8,128)S(1)}, f32[192,1536]{1,0:T(8,128)}, u32[]{:S(2)}) copy-start(f32[192,1536]{1,0:T(8,128)} %fusion.22) | copy-start | bytes 3538948
  137.7 1.9 %copy-start.4 = (bf16[192,8,128]{2,0,1:T(8,128)(2,1)S(1)}, bf16[192,8,128]{2,0,1:T(8,128)(2,1)}, u32[]{:S(2)}) copy-start(bf16[192,8,128]{2,0,1:T(8,128)(2,1)} %copy.7) | copy-start | bytes 1179652
  137.7 3.3 %copy-start.7 = (bf16[1536,8,128]{2,0,1:T(8,128)(2,1)S(1)}, bf16[1536,8,128]{2,0,1:T(8,128)(2,1)}, u32[]{:S(2)}) copy-start(bf16[1536,8,128]{2,0,1:T(8,128)(2,1)} %all-gather.5.cloned.1.call-done) | copy-start | bytes 9437188
  139.6 1.6 %copy-start.2 = (f32[192,1536]{1,0:T(8,128)S(1)}, f32[192,1536]{1,0:T(8,128)}, u32[]{:S(2)}) copy-start(f32[192,1536]{1,0:T(8,128)} %fusion.20) | copy-start | bytes 3538948
  141.2 1.3 copy-start.1
  142.5 1.3 copy-start
Sparse Core Ops, SparseCore 0:
  9.6 66.3 all-gather.2
  78.1 59.5 all-gather.4
  147.1 6.0 reduce-scatter.1
where the time goes:
time: 162 us; the launch traced here: 161 us
  waiting for transfers between devices  74.7 us (46%)
  blocking collectives  47.4 us (29%)
  matrix products  17.8 us (11%)
  between operations  13.9 us (9%)
  local copies, waits for them, and re-layouts  5.75 us (4%)
    all_gather x1, waiting for transfers between devices, on_device(): piece_grads = lax.all_gather(grads, 'tok', axis=0, tiled=True)  51 us
    all_gather x1, blocking collectives, on_device(): piece_losses = lax.all_gather(losses, 'tok', axis=0, tiled=True)  34.1 us
    all_gather x1, waiting for transfers between devices, on_device(): piece_acts = lax.all_gather(acts, 'tok', axis=0, tiled=True)  17.5 us
    unnamed x1, blocking collectives  13.3 us
    dot_general x8, matrix products, pair_block(): jnp.einsum('ik,jk->ij', own_acts[:, layer, :], other_acts[:, layer, :], p...  10.7 us
    reduce_scatter x1, waiting for transfers between devices, on_device(): lax.psum_scatter(partial_scores.astype(jnp.bfloat16), 'lay', scatter_dime...  6.2 us
    unnamed x29, local copies, waits for them, and re-layouts  5.67 us
    dot_general x7, matrix products, pair_block(): jnp.einsum('ik,jk->ij', own_grads[:, layer, :], other_grads[:, layer, :],...  4.84 us
  transfers between devices with their start and end apart: 3, of which 3 were waited for; matrix products, arithmetic and copies ran while one was open for 8% of the time, Pallas kernels for 0%

commit v1 on v0

v1 whole, which is shorter than its diff:
```python
import functools
import math

import jax
import jax.numpy as jnp
from jax import lax
from jax.experimental import pallas as pl
from jax.experimental.pallas import tpu as pltpu
from jax.sharding import PartitionSpec as P

MESH = pl.DeviceIdType.MESH
F32 = jnp.float32
BF16 = jnp.bfloat16
GROUP = 2


def nt(a, b):
    return lax.dot_general(a, b, (((1,), (1,)), ((), ())), preferred_element_type=F32)


def kernel(
    n, lh, scale,
    acts, grads, losses, sources, out,
    stage, send, recv, lall, srcs, total, xsend, xrecv, rsend, rrecv,
    send_sem, recv_sem, ls_sem, lr_sem, lf_sem, lx_sem, ly_sem, ss_sem, sr_sem,
    xs_sem, xr_sem, rs_sem, rr_sem,
):
    block = acts.shape[0]
    half = block // 2
    sets = n // lh
    me = lax.axis_index("tok")
    h = lax.axis_index("lay")
    q, j = me // lh, lax.rem(me, lh)

    def dest(k):
        return lax.rem(q + sets - k // lh, sets) * lh + jnp.bitwise_xor(j, k % lh)

    mine = pl.ds(pl.multiple_of(h * half, half), half)
    theirs = pl.ds(pl.multiple_of((1 - h) * half, half), half)
    peers = list(range(1, n))
    order = sorted(range(1, lh), key=lambda k: (-(k.bit_length()), k))
    send_order = [kq * lh + kj for kj in order for kq in range(sets)] + [kq * lh for kq in range(1, sets)]

    barrier = pltpu.get_barrier_semaphore()
    for k in peers:
        pl.semaphore_signal(barrier, inc=1, device_id={"tok": dest(k)}, device_id_type=MESH)
    pl.semaphore_signal(barrier, inc=1, device_id={"lay": 1 - h}, device_id_type=MESH)

    for w, ref in enumerate((acts, grads)):
        stage[w] = ref[...].astype(F32).reshape(block * lh, ref.shape[2])
    lall[0] = losses[...]
    srcs[0] = sources[...]
    pl.semaphore_wait(barrier, n)

    def remote(src, dst, s, r, **where):
        return pltpu.make_async_remote_copy(
            src_ref=src, dst_ref=dst, send_sem=s, recv_sem=r, device_id=where, device_id_type=MESH
        )

    copies = []

    def go(copy):
        copy.start()
        copies.append(copy)
        return copy

    first = {}
    for k in send_order:
        if k % 2 == 0:
            first[k] = go(remote(losses.at[mine], lall.at[k, mine], ls_sem.at[k], lr_sem.at[k], tok=dest(k)))
    first[1] = go(remote(losses.at[mine], lall.at[1, mine], ls_sem.at[1], lr_sem.at[1], tok=dest(1)))
    ids = {}
    for k in send_order:
        ids[k] = go(remote(sources, srcs.at[k], ss_sem.at[k], sr_sem.at[k], tok=dest(k)))
    main = {}
    for kj in order + [0]:
        layer = jnp.bitwise_xor(j, kj)
        for w in range(2):
            piece = stage[w, pl.ds(layer, block, stride=lh), :].astype(BF16)
            send[kj, w] = piece
            if kj == 0:
                recv[0, w] = piece
        for kq in range(sets):
            k = kq * lh + kj
            if k:
                main[k] = go(remote(send.at[kj], recv.at[k], send_sem.at[k], recv_sem.at[k], tok=dest(k)))

    cross = {}
    for k in range(1, n):
        if k % 2 == 0:
            first[k].wait_recv()
            first[k + 1] = go(
                remote(lall.at[k, mine], lall.at[k + 1, mine], lf_sem.at[k + 1], lr_sem.at[k + 1], tok=dest(1))
            )
            cross[k] = go(remote(lall.at[k, mine], lall.at[k, mine], lx_sem.at[k], ly_sem.at[k], lay=1 - h))
    for k in range(1, n):
        if k % 2 == 1:
            first[k].wait_recv()
            cross[k] = go(remote(lall.at[k, mine], lall.at[k, mine], lx_sem.at[k], ly_sem.at[k], lay=1 - h))

    size = GROUP * block
    flat = (size, acts.shape[2])

    def part(ref_slice):
        return ref_slice.reshape(flat)

    def arrive(g):
        for k in range(g * GROUP, (g + 1) * GROUP):
            if k:
                main[k].wait_recv()
                ids[k].wait_recv()
                cross[k].wait_recv()

    def row_ids(g):
        return jnp.concatenate([srcs[g * GROUP + i] for i in range(GROUP)], axis=1)

    rows = {}
    cols = {}

    def one(a, b):
        sa, sb = pl.ds(a * GROUP, GROUP), pl.ds(b * GROUP, GROUP)
        x = nt(part(recv[sa, 0]), part(recv[sb, 0])) * nt(part(recv[sa, 1]), part(recv[sb, 1]))
        col = cols[a]
        reps = size // col.shape[1]
        keep = jnp.concatenate([col] * reps, axis=1) != rows[b]
        x = jnp.where(keep, x, 0.0).astype(BF16)
        return jnp.dot(x, lall[sb].reshape(size, losses.shape[1]), preferred_element_type=F32)

    groups = lh // GROUP
    for g in range(groups):
        arrive(g)
        rows[g] = row_ids(g)
        cols[g] = jnp.broadcast_to(rows[g], (128, size)).T
        acc = one(g, 0)
        for b in range(1, g + 1):
            acc = acc + one(g, b)
        total[pl.ds(g * GROUP, GROUP)] = acc.reshape(GROUP, block, losses.shape[1])
        for a in range(g):
            total[pl.ds(a * GROUP, GROUP)] += one(a, g).reshape(GROUP, block, losses.shape[1])
    for g in range(groups, n // GROUP):
        arrive(g)
    if sets > 1:
        for a in range(groups):
            cols[a] = cols[a]

        @pl.loop(groups, n // GROUP)
        def _(g):
            rows[-1] = jnp.concatenate([srcs[g * GROUP + i] for i in range(GROUP)], axis=1)
            sb = pl.ds(g * GROUP, GROUP)
            for a in range(groups):
                sa = pl.ds(a * GROUP, GROUP)
                x = nt(part(recv[sa, 0]), part(recv[sb, 0])) * nt(part(recv[sa, 1]), part(recv[sb, 1]))
                col = jnp.broadcast_to(row_ids(a), (128, size)).T
                keep = jnp.concatenate([col] * (size // 128), axis=1) != rows[-1]
                x = jnp.where(keep, x, 0.0).astype(BF16)
                y = jnp.dot(x, lall[sb].reshape(size, losses.shape[1]), preferred_element_type=F32)
                total[sa] += y.reshape(GROUP, block, losses.shape[1])

    xsend[...] = total[:, theirs].astype(BF16)
    swap = go(remote(xsend, xrecv, xs_sem, xr_sem, lay=1 - h))
    swap.wait_recv()
    back = []
    for kj in order:
        rsend[kj] = (total[kj, mine] + xrecv[kj].astype(F32)).astype(BF16)
        back.append(
            go(remote(rsend.at[kj], rrecv.at[kj], rs_sem.at[kj], rr_sem.at[kj], tok=dest(kj)))
        )
    acc = total[0, mine] + xrecv[0].astype(F32)
    for kj, copy in zip(order, back):
        copy.wait_recv()
        acc = acc + rrecv[kj].astype(F32)
    out[...] = acc * scale
    for copy in copies:
        copy.wait_send()


def on_device(acts, grads, losses, sources):
    block, lh, width = acts.shape
    dom = losses.shape[1]
    n = lax.axis_size("tok")
    layers = lh * lax.axis_size("lay")
    scale = 1.0 / math.sqrt(n * block * layers)
    half = block // 2
    dma = pltpu.SemaphoreType.DMA
    vmem = pl.BlockSpec(memory_space=pltpu.VMEM)
    pairs = n * block * block * lh
    return pl.pallas_call(
        functools.partial(kernel, n, lh, scale),
        out_shape=jax.ShapeDtypeStruct((half, dom), F32),
        in_specs=[vmem] * 4,
        out_specs=vmem,
        scratch_shapes=[
            pltpu.VMEM((2, block * lh, width), F32),
            pltpu.VMEM((lh, 2, block, width), BF16),
            pltpu.VMEM((n, 2, block, width), BF16),
            pltpu.VMEM((n, block, dom), BF16),
            pltpu.VMEM((n, 1, block), jnp.int32),
            pltpu.VMEM((lh, block, dom), F32),
            pltpu.VMEM((lh, half, dom), BF16),
            pltpu.VMEM((lh, half, dom), BF16),
            pltpu.VMEM((lh, half, dom), BF16),
            pltpu.VMEM((lh, half, dom), BF16),
            dma((n,)), dma((n,)), dma((n,)), dma((n,)), dma((n,)), dma((n,)), dma((n,)), dma((n,)), dma((n,)),
            dma, dma, dma((lh,)), dma((lh,)),
        ],
        compiler_params=pltpu.CompilerParams(
            collective_id=0, has_side_effects=True, vmem_limit_bytes=56 * 1024 * 1024
        ),
        cost_estimate=pl.CostEstimate(
            flops=2 * pairs * (2 * width + dom), bytes_accessed=4 * block * lh * width, transcendentals=0
        ),
    )(acts, grads, losses, sources.reshape(1, block))


def solution(mesh):
    placed = (
        P(("grp", "tok"), "lay", None),
        P(("grp", "tok"), "lay", None),
        P(("grp", "tok"), None),
        P(("grp", "tok")),
    )
    return jax.shard_map(
        on_device,
        mesh=mesh,
        in_specs=placed,
        out_specs=P(("grp", "tok", "lay"), None),
        check_vma=False,
    )
```

time: 162 us -> 39.4 us (0.24)
  waiting for transfers between devices: 74.7 us -> 0 us
  blocking collectives: 47.4 us -> 0 us
  Pallas kernels: 0 us -> 37.8 us
  matrix products: 17.8 us -> 0 us
  between operations: 13.9 us -> 0.01 us
  local copies, waits for them, and re-layouts: 5.75 us -> 1.42 us
    all_gather x2 -> x0, waiting for transfers between devices: 68.5 us -> none  [the longest x1 51 us: on_device(): piece_grads = lax.all_gather(grads, 'tok', axis=0, tiled=True)]
    pallas_call x0 -> x1, Pallas kernels: none -> 37.8 us  [on_device(): pl.pallas_call(functools.partial(kernel, n, lh, scale), out_shape=jax.Sha...]
    all_gather x1 -> x0, blocking collectives: 34.1 us -> none  [on_device(): piece_losses = lax.all_gather(losses, 'tok', axis=0, tiled=True)]
    dot_general x16 -> x0, matrix products: 17.8 us -> none  [the longest x8 10.7 us: pair_block(): jnp.einsum('ik,jk->ij', own_acts[:, layer, :], other_acts[:, layer, :], p...]
    unnamed x1 -> x0, blocking collectives: 13.3 us -> none
    reduce_scatter x1 -> x0, waiting for transfers between devices: 6.2 us -> none  [on_device(): lax.psum_scatter(partial_scores.astype(jnp.bfloat16), 'lay', scatter_dime...]
    unnamed x29 -> x1, local copies, waits for them, and re-layouts: 5.67 us -> 1.42 us
  transfers between devices with their start and end apart: 3 -> 0, of which waited for: 3 -> 0; matrix products, arithmetic and copies ran while one was open for 8% -> 0% of each run, Pallas kernels for 0% -> 0%
where the time goes in v1:
time: 39.4 us; the launch traced here: 39.2 us
  Pallas kernels  37.8 us (96%)
  local copies, waits for them, and re-layouts  1.42 us (4%)
    pallas_call x1, Pallas kernels, on_device(): pl.pallas_call(functools.partial(kernel, n, lh, scale), out_shape=jax.Sha...  37.8 us
    unnamed x1, local copies, waits for them, and re-layouts  1.42 us

profile of v1, /device:TPU:0, one launch (start us, length us, event | category | flops | bytes accessed | tf_op | source)
XLA Modules:
  0.0 39.2 jit_solution(14313699789484242333)
XLA Ops:
  0.0 37.8 %shard_map.46 = f32[96,128]{1,0:T(8,128)} custom-call(bf16[192,8,128]{2,1,0:T(8,128)(2,1)} %acts.1, bf16[192,8,128]{2,1,0:T(8,128)(2,1)} %grads.1, bf16[192,128]{1,0:T(8,128)(2,1)} %losses.1, s32[1,192]{1,0:T(1,128)} %bitcast.1), custom_call_target="tpu_custom_call" | custom-call | flops 1811939328 | bytes 786432 | tf_op jit(solution)/shard_map/pallas_call | solution.py:187
  37.8 1.4 %copy.6 = f32[96,128]{1,0:T(8,128)} copy(f32[96,128]{1,0:T(8,128)} %shard_map.46) | data formatting | bytes 98304

commit v2 on v1

--- a/solution.py
+++ b/solution.py
@@ -21,9 +21,9 @@
 def kernel(
     n, lh, scale,
     acts, grads, losses, sources, out,
-    stage, send, recv, lall, srcs, total, xsend, xrecv, rsend, rrecv,
+    fetched, stage, send, recv, lall, srcs, total, xsend, xrecv, rsend, rrecv,
     send_sem, recv_sem, ls_sem, lr_sem, lf_sem, lx_sem, ly_sem, ss_sem, sr_sem,
-    xs_sem, xr_sem, rs_sem, rr_sem,
+    xs_sem, xr_sem, rs_sem, rr_sem, in_sem,
 ):
     block = acts.shape[0]
     half = block // 2
@@ -46,10 +46,32 @@
         pl.semaphore_signal(barrier, inc=1, device_id={"tok": dest(k)}, device_id_type=MESH)
     pl.semaphore_signal(barrier, inc=1, device_id={"lay": 1 - h}, device_id_type=MESH)
 
-    for w, ref in enumerate((acts, grads)):
-        stage[w] = ref[...].astype(F32).reshape(block * lh, ref.shape[2])
-    lall[0] = losses[...]
-    srcs[0] = sources[...]
+    local = [
+        pltpu.make_async_copy(src, dst, in_sem.at[i])
+        for i, (src, dst) in enumerate(
+            ((acts, fetched.at[0]), (grads, fetched.at[1]), (losses, lall.at[0]), (sources, srcs.at[0]))
+        )
+    ]
+    for copy in local:
+        copy.start()
+
+    def cut(kj):
+        layer = jnp.bitwise_xor(j, kj)
+        for w in range(2):
+            piece = stage[w, pl.ds(layer, block, stride=lh), :].astype(BF16)
+            if kj == 0:
+                recv[0, w] = piece
+            if kj or sets > 1:
+                send[kj, w] = piece
+
+    ready = order[: lh // 2]
+    for w in range(2):
+        local[w].wait()
+        stage[w] = fetched[w].astype(F32).reshape(block * lh, acts.shape[2])
+    for kj in ready:
+        cut(kj)
+    for copy in local[2:]:
+        copy.wait()
     pl.semaphore_wait(barrier, n)
 
     def remote(src, dst, s, r, **where):
@@ -67,19 +89,15 @@
     first = {}
     for k in send_order:
         if k % 2 == 0:
-            first[k] = go(remote(losses.at[mine], lall.at[k, mine], ls_sem.at[k], lr_sem.at[k], tok=dest(k)))
-    first[1] = go(remote(losses.at[mine], lall.at[1, mine], ls_sem.at[1], lr_sem.at[1], tok=dest(1)))
+            first[k] = go(remote(lall.at[0, mine], lall.at[k, mine], ls_sem.at[k], lr_sem.at[k], tok=dest(k)))
+    first[1] = go(remote(lall.at[0, mine], lall.at[1, mine], ls_sem.at[1], lr_sem.at[1], tok=dest(1)))
     ids = {}
     for k in send_order:
-        ids[k] = go(remote(sources, srcs.at[k], ss_sem.at[k], sr_sem.at[k], tok=dest(k)))
+        ids[k] = go(remote(srcs.at[0], srcs.at[k], ss_sem.at[k], sr_sem.at[k], tok=dest(k)))
     main = {}
     for kj in order + [0]:
-        layer = jnp.bitwise_xor(j, kj)
-        for w in range(2):
-            piece = stage[w, pl.ds(layer, block, stride=lh), :].astype(BF16)
-            send[kj, w] = piece
-            if kj == 0:
-                recv[0, w] = piece
+        if kj not in ready:
+            cut(kj)
         for kq in range(sets):
             k = kq * lh + kj
             if k:
@@ -126,49 +144,75 @@
         x = jnp.where(keep, x, 0.0).astype(BF16)
         return jnp.dot(x, lall[sb].reshape(size, losses.shape[1]), preferred_element_type=F32)
 
+    dom = losses.shape[1]
+
+    def add(a, b):
+        total[pl.ds(a * GROUP, GROUP)] += one(a, b).reshape(GROUP, block, dom)
+
+    swaps = {}
+    back = {}
+
+    def swap(a):
+        at = pl.ds(a * GROUP, GROUP)
+        xsend[at] = total[at, theirs].astype(BF16)
+        swaps[a] = go(remote(xsend.at[at], xrecv.at[at], xs_sem.at[a], xr_sem.at[a], lay=1 - h))
+
+    def owners(a):
+        swaps[a].wait_recv()
+        for k in range(a * GROUP, (a + 1) * GROUP):
+            if k:
+                rsend[k] = (total[k, mine] + xrecv[k].astype(F32)).astype(BF16)
+                back[k] = go(remote(rsend.at[k], rrecv.at[k], rs_sem.at[k], rr_sem.at[k], tok=dest(k)))
+
     groups = lh // GROUP
+    last = groups - 1
     for g in range(groups):
         arrive(g)
         rows[g] = row_ids(g)
         cols[g] = jnp.broadcast_to(rows[g], (128, size)).T
+        if g == last and sets == 1:
+            break
         acc = one(g, 0)
         for b in range(1, g + 1):
             acc = acc + one(g, b)
-        total[pl.ds(g * GROUP, GROUP)] = acc.reshape(GROUP, block, losses.shape[1])
+        total[pl.ds(g * GROUP, GROUP)] = acc.reshape(GROUP, block, dom)
         for a in range(g):
-            total[pl.ds(a * GROUP, GROUP)] += one(a, g).reshape(GROUP, block, losses.shape[1])
-    for g in range(groups, n // GROUP):
-        arrive(g)
+            add(a, g)
     if sets > 1:
-        for a in range(groups):
-            cols[a] = cols[a]
+        for g in range(groups, n // GROUP):
+            arrive(g)
 
         @pl.loop(groups, n // GROUP)
         def _(g):
-            rows[-1] = jnp.concatenate([srcs[g * GROUP + i] for i in range(GROUP)], axis=1)
+            there = jnp.concatenate([srcs[g * GROUP + i] for i in range(GROUP)], axis=1)
             sb = pl.ds(g * GROUP, GROUP)
             for a in range(groups):
                 sa = pl.ds(a * GROUP, GROUP)
                 x = nt(part(recv[sa, 0]), part(recv[sb, 0])) * nt(part(recv[sa, 1]), part(recv[sb, 1]))
                 col = jnp.broadcast_to(row_ids(a), (128, size)).T
-                keep = jnp.concatenate([col] * (size // 128), axis=1) != rows[-1]
+                keep = jnp.concatenate([col] * (size // 128), axis=1) != there
                 x = jnp.where(keep, x, 0.0).astype(BF16)
-                y = jnp.dot(x, lall[sb].reshape(size, losses.shape[1]), preferred_element_type=F32)
-                total[sa] += y.reshape(GROUP, block, losses.shape[1])
-
-    xsend[...] = total[:, theirs].astype(BF16)
-    swap = go(remote(xsend, xrecv, xs_sem, xr_sem, lay=1 - h))
-    swap.wait_recv()
-    back = []
-    for kj in order:
-        rsend[kj] = (total[kj, mine] + xrecv[kj].astype(F32)).astype(BF16)
-        back.append(
-            go(remote(rsend.at[kj], rrecv.at[kj], rs_sem.at[kj], rr_sem.at[kj], tok=dest(kj)))
-        )
+                y = jnp.dot(x, lall[sb].reshape(size, dom), preferred_element_type=F32)
+                total[sa] += y.reshape(GROUP, block, dom)
+
+    turn = sorted(range(groups), key=lambda a: (-(a.bit_length()), a))
+    for i, a in enumerate(turn):
+        if sets == 1:
+            if a == last:
+                acc = one(a, 0)
+                for b in range(1, groups):
+                    acc = acc + one(a, b)
+                total[pl.ds(a * GROUP, GROUP)] = acc.reshape(GROUP, block, dom)
+            else:
+                add(a, last)
+        swap(a)
+        if i:
+            owners(turn[i - 1])
+    owners(turn[-1])
     acc = total[0, mine] + xrecv[0].astype(F32)
-    for kj, copy in zip(order, back):
-        copy.wait_recv()
-        acc = acc + rrecv[kj].astype(F32)
+    for k in order[::-1]:
+        back[k].wait_recv()
+        acc = acc + rrecv[k].astype(F32)
     out[...] = acc * scale
     for copy in copies:
         copy.wait_send()
@@ -187,9 +231,10 @@
     return pl.pallas_call(
         functools.partial(kernel, n, lh, scale),
         out_shape=jax.ShapeDtypeStruct((half, dom), F32),
-        in_specs=[vmem] * 4,
+        in_specs=[pl.BlockSpec(memory_space=pl.ANY)] * 4,
         out_specs=vmem,
         scratch_shapes=[
+            pltpu.VMEM((2, block, lh, width), BF16),
             pltpu.VMEM((2, block * lh, width), F32),
             pltpu.VMEM((lh, 2, block, width), BF16),
             pltpu.VMEM((n, 2, block, width), BF16),
@@ -201,7 +246,7 @@
             pltpu.VMEM((lh, half, dom), BF16),
             pltpu.VMEM((lh, half, dom), BF16),
             dma((n,)), dma((n,)), dma((n,)), dma((n,)), dma((n,)), dma((n,)), dma((n,)), dma((n,)), dma((n,)),
-            dma, dma, dma((lh,)), dma((lh,)),
+            dma((lh,)), dma((lh,)), dma((lh,)), dma((lh,)), dma((4,)),
         ],
         compiler_params=pltpu.CompilerParams(
             collective_id=0, has_side_effects=True, vmem_limit_bytes=56 * 1024 * 1024

time: 39.4 us -> 38 us (0.964)
  Pallas kernels: 37.8 us -> 36.4 us
    pallas_call x1, Pallas kernels: 37.8 us -> 36.4 us  [on_device(): pl.pallas_call(functools.partial(kernel, n, lh, scale), out_shape=jax.Sha...]
where the time goes in v2:
time: 38 us; the launch traced here: 37.8 us
  Pallas kernels  36.4 us (96%)
  local copies, waits for them, and re-layouts  1.42 us (4%)
    pallas_call x1, Pallas kernels, on_device(): pl.pallas_call(functools.partial(kernel, n, lh, scale), out_shape=jax.Sha...  36.4 us
    unnamed x1, local copies, waits for them, and re-layouts  1.42 us

profile of v2, /device:TPU:0, one launch (start us, length us, event | category | flops | bytes accessed | tf_op | source)
XLA Modules:
  0.0 37.8 jit_solution(10423891489339064803)
XLA Ops:
  0.0 36.4 %shard_map.46 = f32[96,128]{1,0:T(8,128)} custom-call(bf16[192,8,128]{2,1,0:T(8,128)(2,1)} %acts.1, bf16[192,8,128]{2,1,0:T(8,128)(2,1)} %grads.1, bf16[192,128]{1,0:T(8,128)(2,1)} %losses.1, s32[1,192]{1,0:T(1,128)} %bitcast.1), custom_call_target="tpu_custom_call" | custom-call | flops 1811939328 | bytes 786432 | tf_op jit(solution)/shard_map/pallas_call | solution.py:231
  36.4 1.4 %copy.6 = f32[96,128]{1,0:T(8,128)} copy(f32[96,128]{1,0:T(8,128)} %shard_map.46) | data formatting | bytes 98304

commit v3 on v2

--- a/solution.py
+++ b/solution.py
@@ -135,19 +135,33 @@
     rows = {}
     cols = {}
 
-    def one(a, b):
+    def one(a, b, both=False):
         sa, sb = pl.ds(a * GROUP, GROUP), pl.ds(b * GROUP, GROUP)
         x = nt(part(recv[sa, 0]), part(recv[sb, 0])) * nt(part(recv[sa, 1]), part(recv[sb, 1]))
         col = cols[a]
         reps = size // col.shape[1]
         keep = jnp.concatenate([col] * reps, axis=1) != rows[b]
         x = jnp.where(keep, x, 0.0).astype(BF16)
-        return jnp.dot(x, lall[sb].reshape(size, losses.shape[1]), preferred_element_type=F32)
+        y = jnp.dot(x, lall[sb].reshape(size, losses.shape[1]), preferred_element_type=F32)
+        if not both:
+            return y
+        z = lax.dot_general(x, lall[sa].reshape(size, losses.shape[1]), (((0,), (0,)), ((), ())), preferred_element_type=F32)
+        return y, z
 
     dom = losses.shape[1]
 
     def add(a, b):
         total[pl.ds(a * GROUP, GROUP)] += one(a, b).reshape(GROUP, block, dom)
+
+    def full(g, after=None):
+        acc = one(g, g)
+        for a in sorted(range(g), key=lambda a: (-(a.bit_length()), a)):
+            y, z = one(a, g, True)
+            total[pl.ds(a * GROUP, GROUP)] += y.reshape(GROUP, block, dom)
+            acc = acc + z
+            if after and a == g - 1:
+                after(a)
+        total[pl.ds(g * GROUP, GROUP)] = acc.reshape(GROUP, block, dom)
 
     swaps = {}
     back = {}
@@ -172,12 +186,7 @@
         cols[g] = jnp.broadcast_to(rows[g], (128, size)).T
         if g == last and sets == 1:
             break
-        acc = one(g, 0)
-        for b in range(1, g + 1):
-            acc = acc + one(g, b)
-        total[pl.ds(g * GROUP, GROUP)] = acc.reshape(GROUP, block, dom)
-        for a in range(g):
-            add(a, g)
+        full(g)
     if sets > 1:
         for g in range(groups, n // GROUP):
             arrive(g)
@@ -197,18 +206,14 @@
 
     turn = sorted(range(groups), key=lambda a: (-(a.bit_length()), a))
     for i, a in enumerate(turn):
-        if sets == 1:
-            if a == last:
-                acc = one(a, 0)
-                for b in range(1, groups):
-                    acc = acc + one(a, b)
-                total[pl.ds(a * GROUP, GROUP)] = acc.reshape(GROUP, block, dom)
-            else:
-                add(a, last)
-        swap(a)
-        if i:
-            owners(turn[i - 1])
-    owners(turn[-1])
+        if i == 0 and sets == 1:
+            full(last, swap)
+            for a in turn[1:]:
+                swap(a)
+        elif sets > 1:
+            swap(a)
+    for a in turn:
+        owners(a)
     acc = total[0, mine] + xrecv[0].astype(F32)
     for k in order[::-1]:
         back[k].wait_recv()

time: 38 us -> 37.4 us (0.984)
  Pallas kernels: 36.4 us -> 35.8 us
    pallas_call x1, Pallas kernels: 36.4 us -> 35.8 us  [on_device(): pl.pallas_call(functools.partial(kernel, n, lh, scale), out_shape=jax.Sha...]
where the time goes in v3:
time: 37.4 us; the launch traced here: 37.2 us
  Pallas kernels  35.8 us (96%)
  local copies, waits for them, and re-layouts  1.42 us (4%)
    pallas_call x1, Pallas kernels, on_device(): pl.pallas_call(functools.partial(kernel, n, lh, scale), out_shape=jax.Sha...  35.8 us
    unnamed x1, local copies, waits for them, and re-layouts  1.42 us

profile of v3, /device:TPU:0, one launch (start us, length us, event | category | flops | bytes accessed | tf_op | source)
XLA Modules:
  0.0 37.2 jit_solution(15010076833832507739)
XLA Ops:
  0.0 35.8 %shard_map.46 = f32[96,128]{1,0:T(8,128)} custom-call(bf16[192,8,128]{2,1,0:T(8,128)(2,1)} %acts.1, bf16[192,8,128]{2,1,0:T(8,128)(2,1)} %grads.1, bf16[192,128]{1,0:T(8,128)(2,1)} %losses.1, s32[1,192]{1,0:T(1,128)} %bitcast.1), custom_call_target="tpu_custom_call" | custom-call | flops 1811939328 | bytes 786432 | tf_op jit(solution)/shard_map/pallas_call | solution.py:236
  35.8 1.4 %copy.6 = f32[96,128]{1,0:T(8,128)} copy(f32[96,128]{1,0:T(8,128)} %shard_map.46) | data formatting | bytes 98304
